TPU v7x, 32 devices: a whole 2x2x4 slice. The times are simulated.
32 devices in a mesh: ctx: 8 (over z, y), exp: 4 (over x, core).
Axes of the slice: x: 2, y: 2, z: 4, core: 2. Of those that a mesh axis runs over, the one named last changes fastest.
Arguments:
- frames: bfloat16 [4, 768, 2048], P('exp', 'ctx'), may hold values from -6 to 6
- queries: bfloat16 [4, 768, 2048], P('exp', 'ctx'), may hold values from -8 to 8
- keys: bfloat16 [4, 768, 2048], P('exp', 'ctx'), may hold values from -8 to 8
- values: bfloat16 [4, 768, 2048], P('exp', 'ctx'), may hold values from -6 to 6
- expert_ids: int32 [4, 768, 2], P('exp', 'ctx'), may hold values from 0 to 7, all different within a row; in each aligned block of 96 rows (0 to 95, 96 to 191, ..., all dimensions but the last counted through in order) at most 48 rows name the same one
- gate_weights: float32 [4, 768, 2], P('exp', 'ctx'), may hold values from 0.2 to 1
- w_in: bfloat16 [8, 2048, 8192], P('exp', None, 'ctx'), may hold values from -0.125 to 0.125
- w_out: bfloat16 [8, 8192, 2048], P('exp', 'ctx'), may hold values from -0.0625 to 0.0625
Outputs:
- layer_out: bfloat16 [4, 768, 2048], P('exp', 'ctx')
Inputs may be any that keep to these rules, and one draw needn't show every extreme that they name: `expert_ids`: each row names two different experts; within the rows of one device no expert is named by more than 48 rows, a bound that some block reaches.
All inputs are finite; a program needn't handle non-finite values.
Results may differ from a plain program's by a relative error of at most 0.013.
Values may be sent and summed in bfloat16 or wider, within the bound.
No kernel may reach another device: no remote copies, remote signals or barrier semaphores. Data moves between devices by JAX's collectives and lax.ppermute only.
A program may use at most 192 MiB of HBM per device.

v0:
```python
import functools
import math

import jax
import jax.numpy as jnp
from jax import lax
from jax.experimental import pallas as pl
from jax.experimental.pallas import tpu as pltpu
from jax.sharding import PartitionSpec as P

HEADS = 16
HD = 128


EPSILON = 1e-05


def gelu_tanh(values_in):
    return jax.nn.gelu(values_in, approximate=True)


def expert_partial(gathered, live_flags, first_w, second_w):
    total_rows = gathered.shape[0]
    out_width = second_w.shape[1]
    padded_rows = -(-total_rows // 128) * 128
    position = jnp.cumsum(live_flags) - 1
    live_count = jnp.sum(live_flags)
    target = jnp.where(live_flags > 0, position, padded_rows)
    order_idx = (
        jnp.zeros((padded_rows,), jnp.int32)
        .at[target]
        .set(jnp.arange(total_rows, dtype=jnp.int32), mode="drop")
    )
    block_count = (live_count + 127) // 128

    def one_block(block_num, packed):
        picked = lax.dynamic_slice_in_dim(order_idx, block_num * 128, 128)
        inputs = jnp.take(gathered, picked, axis=0)
        inner_act = gelu_tanh(jnp.dot(inputs, first_w, preferred_element_type=jnp.float32)).astype(
            jnp.bfloat16
        )
        output = jnp.dot(inner_act, second_w, preferred_element_type=jnp.float32).astype(
            jnp.bfloat16
        )
        return lax.dynamic_update_slice_in_dim(packed, output, block_num * 128, 0)

    packed = lax.fori_loop(
        0, block_count, one_block, jnp.zeros((padded_rows, out_width), jnp.bfloat16)
    )
    back_idx = jnp.where(live_flags > 0, position, 0).astype(jnp.int32)
    unpacked = jnp.take(packed, back_idx, axis=0)
    return jnp.where((live_flags > 0)[:, None], unpacked, jnp.zeros_like(unpacked))


def routed_ffn(hidden_f, normed, expert_ids, gate_weights, w_in, w_out):
    tok_count, model_width = normed.shape
    slot_ids = expert_ids[0].reshape(-1)
    slot_count = slot_ids.shape[0]
    exp_local = w_in.shape[0]
    num_experts = exp_local * lax.axis_size("exp")
    capacity = 2 * (slot_count // num_experts)
    onehot = (slot_ids[:, None] == jnp.arange(num_experts, dtype=jnp.int32)[None, :]).astype(
        jnp.int32
    )
    slot_rank = jnp.sum((jnp.cumsum(onehot, axis=0) - onehot) * onehot, axis=1)
    target = slot_ids * capacity + slot_rank
    send_matrix = (
        jnp.arange(num_experts * capacity, dtype=jnp.int32)[:, None] == target[None, :]
    ).astype(jnp.int32)
    token_matrix = send_matrix.reshape(num_experts * capacity, tok_count, 2).sum(-1)
    outgoing = jnp.dot(
        token_matrix.astype(jnp.bfloat16), normed, preferred_element_type=jnp.float32
    ).astype(jnp.bfloat16)
    outgoing = outgoing.reshape(num_experts, capacity, model_width)
    occupied = jnp.sum(send_matrix, axis=1).reshape(num_experts, capacity)
    arrived, arrived_flags = (
        lax.all_to_all(outgoing, "exp", split_axis=0, concat_axis=1, tiled=True),
        lax.all_to_all(occupied, "exp", split_axis=0, concat_axis=1, tiled=True),
    )
    gathered, gathered_flags = (
        lax.all_gather(arrived, "ctx", axis=1, tiled=True),
        lax.all_gather(arrived_flags, "ctx", axis=1, tiled=True),
    )
    summed_list = []
    for local_num in range(exp_local):
        partial_value = expert_partial(
            gathered[local_num], gathered_flags[local_num], w_in[local_num], w_out[local_num]
        )
        summed_list.append(
            lax.psum_scatter(partial_value, "ctx", scatter_dimension=0, tiled=True)
            .astype(jnp.float32)
            .astype(jnp.bfloat16)
        )
    summed = jnp.stack(summed_list)
    returned = lax.all_to_all(summed, "exp", split_axis=1, concat_axis=0, tiled=True)
    slot_out = jnp.dot(
        send_matrix.T.astype(jnp.bfloat16),
        returned.reshape(num_experts * capacity, model_width),
        preferred_element_type=jnp.float32,
    )
    tok_out = slot_out.reshape(tok_count, 2, model_width)
    gates = gate_weights[0]
    return hidden_f + gates[:, 0:1] * tok_out[:, 0] + gates[:, 1:2] * tok_out[:, 1]


def attend_kernel(q_ref, k_ref, v_ref, o_ref):
    scores = lax.dot_general(
        q_ref[...], k_ref[...], (((1,), (1,)), ((), ())), preferred_element_type=jnp.float32
    ) * (1.0 / math.sqrt(HD))
    raw = jnp.exp(scores - jnp.max(scores, axis=-1, keepdims=True))
    total = jnp.sum(raw, axis=-1, keepdims=True)
    mixed = jnp.dot(raw.astype(jnp.bfloat16), v_ref[...], preferred_element_type=jnp.float32)
    o_ref[...] = (mixed / total).astype(o_ref.dtype)


def attend_heads(packed, local_heads):
    frames = packed.shape[0]
    rows = 256
    return pl.pallas_call(
        attend_kernel,
        grid=(local_heads, frames // rows),
        in_specs=[
            pl.BlockSpec((rows, HD), lambda h, i: (i, h)),
            pl.BlockSpec((frames, HD), lambda h, i: (0, local_heads + h)),
            pl.BlockSpec((frames, HD), lambda h, i: (0, 2 * local_heads + h)),
        ],
        out_specs=pl.BlockSpec((rows, HD), lambda h, i: (i, h)),
        out_shape=jax.ShapeDtypeStruct((frames, local_heads * HD), jnp.bfloat16),
        compiler_params=pltpu.CompilerParams(vmem_limit_bytes=24 << 20),
        cost_estimate=pl.CostEstimate(
            flops=4 * local_heads * frames * frames * HD,
            bytes_accessed=8 * frames * local_heads * HD,
            transcendentals=local_heads * frames * frames,
        ),
        name="attend_heads",
    )(packed, packed, packed)


def attention(queries, keys, values):
    n_ctx = lax.axis_size("ctx")
    tok_count, width = queries.shape
    local_heads = HEADS // n_ctx
    piece = width // n_ctx
    outgoing = jnp.concatenate(
        [jnp.transpose(a.reshape(tok_count, n_ctx, piece), (1, 0, 2)) for a in (queries, keys, values)],
        axis=-1,
    )
    arrived = lax.all_to_all(outgoing, "ctx", split_axis=0, concat_axis=0, tiled=True)
    mixed = attend_heads(arrived.reshape(n_ctx * tok_count, 3 * piece), local_heads)
    returned = lax.all_to_all(
        mixed.reshape(n_ctx, tok_count, piece), "ctx", split_axis=0, concat_axis=0, tiled=True
    )
    return jnp.transpose(returned, (1, 0, 2)).reshape(tok_count, width)


def swap_core(a):
    return lax.ppermute(a, "exp", [(i, i ^ 1) for i in range(4)])


def swap_x(a):
    return lax.ppermute(a, "exp", [(i, i ^ 2) for i in range(4)])


def swap_y(a):
    return lax.ppermute(a, "ctx", [(i, i ^ 1) for i in range(8)])


def turn_z(a, steps):
    return lax.ppermute(a, "ctx", [(i, (i + 2 * steps) % 8) for i in range(8)])


def ffn_kernel(rows_ref, gate_ref, first_ref, second_ref, out_ref, act_ref):
    n_exp, width, inner = first_ref.shape
    cut = 512
    per = inner // cut
    gates = gate_ref[...].T

    @pl.loop(0, n_exp * per)
    def _(i):
        e, j = i // per, i % per
        cols = pl.ds(pl.multiple_of(j * cut, cut), cut)
        factor = gates[:, 0:1]
        for k in range(1, n_exp):
            factor = jnp.where(e == k, gates[:, k : k + 1], factor)
        act = gelu_tanh(
            jnp.dot(rows_ref[...], first_ref[e, :, cols], preferred_element_type=jnp.float32)
        )
        spot = pl.ds(pl.multiple_of(i * cut, cut), cut)
        act_ref[:, spot] = (act * factor).astype(act_ref.dtype)

    @pl.loop(0, width // cut)
    def _(i):
        cols = pl.ds(pl.multiple_of(i * cut, cut), cut)
        out_ref[:, cols] = jnp.dot(
            act_ref[...], second_ref[:, cols], preferred_element_type=jnp.float32
        ).astype(out_ref.dtype)


def gated_ffn(rows, gate, first_w, second_w):
    count, width = rows.shape
    n_exp, hidden = gate.shape[0], second_w.shape[0]
    vmem = pl.BlockSpec(memory_space=pltpu.VMEM)
    return pl.pallas_call(
        ffn_kernel,
        in_specs=[vmem] * 4,
        out_specs=vmem,
        out_shape=jax.ShapeDtypeStruct((count, width), jnp.bfloat16),
        scratch_shapes=[pltpu.VMEM((count, hidden), jnp.bfloat16)],
        compiler_params=pltpu.CompilerParams(vmem_limit_bytes=24 << 20),
        cost_estimate=pl.CostEstimate(
            flops=4 * count * width * hidden,
            bytes_accessed=4 * count * width,
            transcendentals=count * hidden,
        ),
        name="gated_ffn",
    )(rows, jnp.pad(gate, ((0, -n_exp % 8), (0, 0))), first_w, second_w)


def dense_sum(hidden_f, normed, expert_ids, gate_weights, w_in, w_out):
    tok_count, _ = normed.shape
    half = tok_count // 2
    n_local = w_in.shape[0]
    first_w, second_w = w_in, w_out
    f32, bf16 = jnp.float32, jnp.bfloat16
    small = jnp.concatenate([expert_ids[0].astype(f32).T, gate_weights[0].T], axis=0)
    small = jnp.stack([small, swap_y(small)])
    small = jnp.concatenate([small, swap_x(small)])
    small = jnp.stack([small, swap_core(small)])
    small = [small] + [turn_z(small, k) for k in range(1, 4)]
    local_ids = (
        lax.axis_index("exp") * n_local + jnp.arange(n_local, dtype=jnp.int32)
    ).astype(f32)

    def gate_of(slot, core):
        picked = small[slot][core]
        ids = jnp.transpose(picked[:, 0:2], (1, 0, 2)).reshape(2, -1)
        gates = jnp.transpose(picked[:, 2:4], (1, 0, 2)).reshape(2, -1)
        return jnp.sum(
            jnp.where(ids[None] == local_ids[:, None, None], gates[None], 0.0), axis=1
        )

    def neighbours(rows):
        return [rows, swap_y(rows), swap_x(rows)]

    def corners(near):
        return [swap_x(near[1][:half]), swap_y(near[2][half:])]

    def rows_of(near, corner):
        return jnp.concatenate(near + corner)

    def split(own_out, crossed):
        both = own_out.astype(f32) + crossed.astype(f32)
        mine, to_y, to_x = (both[i * tok_count : (i + 1) * tok_count] for i in range(3))
        last = both[3 * tok_count :].astype(bf16)
        return mine, to_y, to_x, swap_x(last[:half]), swap_y(last[half:])

    def pass_on(parts):
        mine, to_y, to_x, from_x, from_y = parts
        to_y = to_y.at[:half].add(from_x.astype(f32)).astype(bf16)
        to_x = to_x.at[half:].add(from_y.astype(f32)).astype(bf16)
        return mine, swap_y(to_y), swap_x(to_x)

    def turn_back_y(own_out, crossed):
        both = own_out.astype(f32) + crossed.astype(f32)
        mine, to_y, to_x, last = (both[i * tok_count : (i + 1) * tok_count] for i in range(4))
        return mine, to_x, swap_y(jnp.concatenate([to_y, last]).astype(bf16))

    def finish(slot, flow):
        plane = flow[0]
        for arrived in flow[1:]:
            plane = plane + arrived.astype(f32)
        return turn_z(plane.astype(bf16), -slot) if slot else plane

    state = {"ring1": turn_z(normed, 1), "near0": neighbours(normed)}

    wide, narrow = (0, 1), ()

    def act(name, slot, *operands):
        key = f"{name}{slot}"
        if name == "ring":
            state[key] = turn_z(*operands, 1)
        elif name == "near":
            state[key] = neighbours(*operands)
        elif name == "corner":
            state[key] = corners(*operands)
        elif name == "y":
            state[key] = swap_y(*operands)
        elif name == "x":
            state[key] = swap_x(jnp.concatenate(operands))
        elif name == "own":
            state[key] = rows_of(*operands) if slot in wide else jnp.concatenate(operands)
            state[f"other{slot}"] = swap_core(state[key])
        elif name == "cross":
            state[key] = swap_core(*operands)
        elif name == "parts":
            state[key] = split(*operands)
        elif name == "back_y":
            state[key] = turn_back_y(*operands)
        elif name == "back_x":
            mine, to_x, arrived = operands[0]
            mine = mine + arrived[:tok_count].astype(f32)
            state[key] = mine, swap_x((to_x + arrived[tok_count:].astype(f32)).astype(bf16))
        elif name == "flow":
            state[key] = pass_on(*operands)
        elif name == "plane":
            state[key] = finish(slot, *operands)

    needs = {
        "ring": lambda k: [f"ring{k - 1}"],
        "near": lambda k: [f"ring{k}"],
        "corner": lambda k: [f"near{k}"],
        "y": lambda k: [f"ring{k}"],
        "x": lambda k: [f"ring{k}", f"y{k}"],
        "own": lambda k: [f"near{k}", f"corner{k}"] if k in wide else [f"ring{k}", f"y{k}", f"x{k}"],
        "cross": lambda k: [f"other_out{k}"],
        "parts": lambda k: [f"own_out{k}", f"cross{k}"],
        "flow": lambda k: [f"parts{k}"],
        "back_y": lambda k: [f"own_out{k}", f"cross{k}"],
        "back_x": lambda k: [f"back_y{k}"],
        "plane": lambda k: [f"back_x{k}"] if k in narrow else [f"flow{k}"],
    }
    steps = [
        None, None, ("own", 0), None,
        ("own", 1), ("other", 1), ("own", 2), ("other", 2),
        ("own", 3), ("other", 3), ("other", 0),
        None, None, None, None,
    ]
    events = [
        [],
        [("corner", 0), ("near", 1), ("ring", 2)],
        [("own", 0)],
        [("corner", 1), ("y", 2), ("ring", 3)],
        [("own", 1), ("x", 2)],
        [("y", 3)],
        [("own", 2), ("cross", 1), ("x", 3)],
        [("parts", 1)],
        [("own", 3), ("cross", 2), ("flow", 1)],
        [("parts", 2), ("plane", 1)],
        [("cross", 3), ("flow", 2)],
        [("parts", 3), ("cross", 0), ("plane", 2)],
        [("flow", 3), ("parts", 0)],
        [("plane", 3), ("flow", 0)],
        [("plane", 0)],
    ]
    due = {1: ["ring1"], 11: ["plane1"], 14: ["plane2"]}
    for number, step in enumerate(steps):
        if number:
            keys = {key for name, slot in events[number] for key in needs[name](slot)}
            keys |= set(due.get(number, []))
            if steps[number - 1]:
                keys.add("{}_out{}".format(*steps[number - 1]))
            if step:
                keys.add("{}{}".format(*step))
            keys = sorted(keys & set(state))
            state.update(zip(keys, lax.optimization_barrier([state[key] for key in keys])))
        for name, slot in events[number]:
            act(name, slot, *(state[key] for key in needs[name](slot)))
        if step:
            which, k = step
            state[f"{which}_out{k}"] = gated_ffn(
                state[f"{which}{k}"], gate_of(k, int(which == "other")), first_w, second_w
            )
    total = hidden_f
    for k in range(4):
        total = total + state[f"plane{k}"].astype(f32)
    return total


def on_device(frames, queries, keys, values, expert_ids, gate_weights, w_in, w_out):
    dense = lax.axis_size("ctx") == 8 and lax.axis_size("exp") == 4
    if dense:
        w_in = pltpu.with_memory_space_constraint(w_in, pltpu.VMEM)
        w_out = pltpu.with_memory_space_constraint(
            w_out.reshape(-1, w_out.shape[-1]), pltpu.VMEM
        )
    attended = attention(queries[0], keys[0], values[0])
    attended = attended.astype(jnp.float32)
    hidden_state = (frames[0].astype(jnp.float32) + attended).astype(jnp.bfloat16)
    hidden_f = hidden_state.astype(jnp.float32)
    normed = (
        hidden_f * lax.rsqrt(jnp.mean(hidden_f * hidden_f, axis=-1, keepdims=True) + EPSILON)
    ).astype(jnp.bfloat16)
    ffn = dense_sum if dense else routed_ffn
    layer_out = ffn(hidden_f, normed, expert_ids, gate_weights, w_in, w_out)
    return layer_out.astype(jnp.bfloat16)[None]


def solution(mesh):
    rows = P("exp", "ctx", None)
    in_specs = (rows,) * 6 + (P("exp", None, "ctx"), P("exp", "ctx", None))
    return jax.shard_map(
        on_device, mesh=mesh, in_specs=in_specs, out_specs=rows, check_vma=False
    )
```

profile of v0, /device:TPU:0, one launch (start us, length us, event | category | flops | bytes accessed | tf_op | source)
XLA Modules:
  0.0 237.2 jit_solution(10589365985223727745)
XLA Ops:
  3.7 7.4 %all-to-all-start = ((bf16[8,96,768]{2,1,0:T(8,128)(2,1)}), bf16[8,96,768]{2,1,0:T(8,128)(2,1)S(1)}, u32[]{:S(2)}, u32[]{:S(2)}) async-start(bf16[8,96,768]{2,1,0:T(8,128)(2,1)} %pad_maximum_fusion), calls=%async_computation | async-start | bytes 2359296 | tf_op jit(solution)/shard_map/all_to_all | solution.py:148
  11.2 2.1 collective-permute-start.8
  13.2 5.9 %collective-permute-done.8 = f32[4,96]{1,0:T(4,128)S(1)} collective-permute-done((f32[4,96]{1,0:T(4,128)S(1)}, f32[4,96]{1,0:T(4,128)S(1)}, u32[]{:S(2)}, u32[]{:S(2)}) %collective-permute-start.8) | collective-permute-done | bytes 1568 | tf_op jit(solution)/shard_map/ppermute | solution.py:165
  20.6 2.1 collective-permute-done.9
  23.9 3.5 %collective-permute-start.16 = (f32[2,4,4,96]{3,2,1,0:T(4,128)S(1)}, f32[2,4,4,96]{3,2,1,0:T(4,128)S(1)}, u32[]{:S(2)}, u32[]{:S(2)}) collective-permute-start(f32[2,4,4,96]{3,2,1,0:T(4,128)S(1)} %pad_maximum_fusion.3), channel_id=1, source_target_pairs={{0,8},{4,12},{8,16},{12,20},{16,24},{20,28},{24,0},{28,4},{1,9},{5... | collective-permute-start | bytes 36872 | tf_op jit(solution)/shard_map/ppermute | solution.py:169
  27.5 2.1 collective-permute-start.22
  31.3 9.4 %all-to-all-done = bf16[8,96,768]{2,1,0:T(8,128)(2,1)S(1)} async-done(((bf16[8,96,768]{2,1,0:T(8,128)(2,1)}), bf16[8,96,768]{2,1,0:T(8,128)(2,1)S(1)}, u32[]{:S(2)}, u32[]{:S(2)}) %all-to-all-start) | async-done | bytes 1179680 | tf_op jit(solution)/shard_map/all_to_all | solution.py:148
  40.7 4.9 %attend_heads.1 = bf16[768,256]{1,0:T(8,128)(2,1)} custom-call(bf16[768,768]{1,0:T(8,128)(2,1)S(1)} %bitcast.86, bf16[768,768]{1,0:T(8,128)(2,1)S(1)} %bitcast.87, bf16[768,768]{1,0:T(8,128)(2,1)S(1)} %bitcast.88), custom_call_target="tpu_custom_call" | custom-call | flops 603979776 | bytes 1572864 | tf_op jit(solution)/shard_map/attend_heads/pallas_call | solution.py:119
  45.6 3.5 %all-to-all-start.1 = ((bf16[8,96,256]{2,1,0:T(8,128)(2,1)}), bf16[8,96,256]{2,1,0:T(8,128)(2,1)S(1)}, u32[]{:S(2)}, u32[]{:S(2)}) async-start(bf16[8,96,256]{2,1,0:T(8,128)(2,1)} %bitcast.5), calls=%async_computation.1 | async-start | bytes 786432 | tf_op jit(solution)/shard_map/all_to_all | solution.py:150
  49.4 11.4 %all-to-all-done.1 = bf16[8,96,256]{2,1,0:T(8,128)(2,1)S(1)} async-done(((bf16[8,96,256]{2,1,0:T(8,128)(2,1)}), bf16[8,96,256]{2,1,0:T(8,128)(2,1)S(1)}, u32[]{:S(2)}, u32[]{:S(2)}) %all-to-all-start.1) | async-done | bytes 393248 | tf_op jit(solution)/shard_map/all_to_all | solution.py:150
  64.3 6.8 %collective-permute-done = bf16[96,2048]{1,0:T(8,128)(2,1)S(1)} collective-permute-done((bf16[96,2048]{1,0:T(8,128)(2,1)S(1)}, bf16[96,2048]{1,0:T(8,128)(2,1)S(1)}, u32[]{:S(2)}, u32[]{:S(2)}) %collective-permute-start) | collective-permute-done | bytes 393248 | tf_op jit(solution)/shard_map/ppermute | solution.py:165
  72.6 3.0 %collective-permute-done.2 = bf16[96,2048]{1,0:T(8,128)(2,1)S(1)} collective-permute-done((bf16[96,2048]{1,0:T(8,128)(2,1)S(1)}, bf16[96,2048]{1,0:T(8,128)(2,1)S(1)}, u32[]{:S(2)}, u32[]{:S(2)}) %collective-permute-start.2) | collective-permute-done | bytes 393248 | tf_op jit(solution)/shard_map/ppermute | solution.py:169
  81.2 2.3 collective-permute-done.3
  84.3 3.4 %copy-done = bf16[2,2048,1024]{2,1,0:T(8,128)(2,1)S(1)} copy-done((bf16[2,2048,1024]{2,1,0:T(8,128)(2,1)S(1)}, bf16[2,2048,1024]{2,1,0:T(8,128)(2,1)}, u32[]{:S(2)}) %copy-start) | copy-done | bytes 8388632
  87.7 3.4 %copy-done.1 = bf16[2,1024,2048]{2,1,0:T(8,128)(2,1)S(1)} copy-done((bf16[2,1024,2048]{2,1,0:T(8,128)(2,1)S(1)}, bf16[2,1024,2048]{2,1,0:T(8,128)(2,1)}, u32[]{:S(2)}) %copy-start.1) | copy-done | bytes 8388632
  91.1 8.8 %gated_ffn.8 = bf16[384,2048]{1,0:T(8,128)(2,1)S(1)} custom-call(bf16[384,2048]{1,0:T(8,128)(2,1)S(1)} %constant_dynamic-update-slice_fusion.rows_ref, f32[8,384]{1,0:T(8,128)S(1)} %pad.41.gate_ref, bf16[2,2048,1024]{2,1,0:T(8,128)(2,1)S(1)} %copy-done, bf16[2048,2048]{1,0:T(8,128)(2,1)S(1)} %bitcast.91), custom_call_target="tpu_custom_call" | custom-call | flops 6442450944 | bytes 3145728 | tf_op jit(solution)/shard_map/gated_ffn/pallas_call | solution.py:203
  101.8 1.8 collective-permute-start.12
  103.6 2.4 collective-permute-done.11
  106.0 3.8 %collective-permute-done.12 = bf16[48,2048]{1,0:T(8,128)(2,1)S(1)} collective-permute-done((bf16[48,2048]{1,0:T(8,128)(2,1)S(1)}, bf16[48,2048]{1,0:T(8,128)(2,1)S(1)}, u32[]{:S(2)}, u32[]{:S(2)}) %collective-permute-start.12) | collective-permute-done | bytes 196640 | tf_op jit(solution)/shard_map/ppermute | solution.py:165
  112.0 8.8 %gated_ffn.9 = bf16[384,2048]{1,0:T(8,128)(2,1)S(1)} custom-call(bf16[384,2048]{1,0:T(8,128)(2,1)S(1)} %constant_dynamic-update-slice_fusion.5.rows_ref, f32[8,384]{1,0:T(8,128)S(1)} %pad.42.gate_ref, bf16[2,2048,1024]{2,1,0:T(8,128)(2,1)S(1)} %copy-done, bf16[2048,2048]{1,0:T(8,128)(2,1)S(1)} %bitcast.92), custom_call_target="tpu_custom_call" | custom-call | flops 6442450944 | bytes 3145728 | tf_op jit(solution)/shard_map/gated_ffn/pallas_call | solution.py:203
  120.7 2.9 %collective-permute-done.17 = bf16[96,2048]{1,0:T(8,128)(2,1)S(1)} collective-permute-done((bf16[96,2048]{1,0:T(8,128)(2,1)S(1)}, bf16[96,2048]{1,0:T(8,128)(2,1)S(1)}, u32[]{:S(2)}, u32[]{:S(2)}) %collective-permute-start.17) | collective-permute-done | bytes 393248 | tf_op jit(solution)/shard_map/ppermute | solution.py:169
  123.9 8.8 %gated_ffn.10 = bf16[384,2048]{1,0:T(8,128)(2,1)S(1)} custom-call(bf16[384,2048]{1,0:T(8,128)(2,1)S(1)} %collective-permute-done.14.rows_ref, f32[8,384]{1,0:T(8,128)S(1)} %pad.43.gate_ref, bf16[2,2048,1024]{2,1,0:T(8,128)(2,1)S(1)} %copy-done, bf16[2048,2048]{1,0:T(8,128)(2,1)S(1)} %bitcast.93), custom_call_target="tpu_custom_call" | custom-call | flops 6442450944 | bytes 3145728 | tf_op jit(solution)/shard_map/gated_ffn/pallas_call | solution.py:203
  137.5 8.8 %gated_ffn.11 = bf16[384,2048]{1,0:T(8,128)(2,1)S(1)} custom-call(bf16[384,2048]{1,0:T(8,128)(2,1)S(1)} %constant_dynamic-update-slice_fusion.10.rows_ref, f32[8,384]{1,0:T(8,128)S(1)} %pad.44.gate_ref, bf16[2,2048,1024]{2,1,0:T(8,128)(2,1)S(1)} %copy-done, bf16[2048,2048]{1,0:T(8,128)(2,1)S(1)} %bitcast.94), custom_call_target="tpu_custom_call" | custom-call | flops 6442450944 | bytes 3145728 | tf_op jit(solution)/shard_map/gated_ffn/pallas_call | solution.py:203
  147.9 8.7 %gated_ffn.12 = bf16[384,2048]{1,0:T(8,128)(2,1)S(1)} custom-call(bf16[384,2048]{1,0:T(8,128)(2,1)S(1)} %collective-permute-done.21.rows_ref, f32[8,384]{1,0:T(8,128)S(1)} %pad.45.gate_ref, bf16[2,2048,1024]{2,1,0:T(8,128)(2,1)S(1)} %bitcast.90, bf16[2048,2048]{1,0:T(8,128)(2,1)S(1)} %bitcast.95), custom_call_target="tpu_custom_call" | custom-call | flops 6442450944 | bytes 3145728 | tf_op jit(solution)/shard_map/gated_ffn/pallas_call | solution.py:203
  156.8 3.1 %collective-permute-done.23 = bf16[48,2048]{1,0:T(8,128)(2,1)S(1)} collective-permute-done((bf16[48,2048]{1,0:T(8,128)(2,1)S(1)}, bf16[48,2048]{1,0:T(8,128)(2,1)S(1)}, u32[]{:S(2)}, u32[]{:S(2)}) %collective-permute-start.23) | collective-permute-done | bytes 196640 | tf_op jit(solution)/shard_map/ppermute | solution.py:161
  163.0 8.7 %gated_ffn.13 = bf16[384,2048]{1,0:T(8,128)(2,1)S(1)} custom-call(bf16[384,2048]{1,0:T(8,128)(2,1)S(1)} %constant_dynamic-update-slice_fusion.13.rows_ref, f32[8,384]{1,0:T(8,128)S(1)} %pad.46.gate_ref, bf16[2,2048,1024]{2,1,0:T(8,128)(2,1)S(1)} %bitcast.90, bf16[2048,2048]{1,0:T(8,128)(2,1)S(1)} %bitcast.96), custom_call_target="tpu_custom_call" | custom-call | flops 6442450944 | bytes 3145728 | tf_op jit(solution)/shard_map/gated_ffn/pallas_call | solution.py:203
  176.7 8.7 %gated_ffn.14 = bf16[384,2048]{1,0:T(8,128)(2,1)S(1)} custom-call(bf16[384,2048]{1,0:T(8,128)(2,1)S(1)} %collective-permute-done.29.rows_ref, f32[8,384]{1,0:T(8,128)S(1)} %pad.47.gate_ref, bf16[2,2048,1024]{2,1,0:T(8,128)(2,1)S(1)} %bitcast.90, bf16[2048,2048]{1,0:T(8,128)(2,1)S(1)} %bitcast.97), custom_call_target="tpu_custom_call" | custom-call | flops 6442450944 | bytes 3145728 | tf_op jit(solution)/shard_map/gated_ffn/pallas_call | solution.py:203
  188.6 8.7 %gated_ffn.15 = bf16[384,2048]{1,0:T(8,128)(2,1)S(1)} custom-call(bf16[384,2048]{1,0:T(8,128)(2,1)S(1)} %collective-permute-done.5.rows_ref, f32[8,384]{1,0:T(8,128)S(1)} %pad.48.gate_ref, bf16[2,2048,1024]{2,1,0:T(8,128)(2,1)S(1)} %bitcast.90, bf16[2048,2048]{1,0:T(8,128)(2,1)S(1)} %bitcast.98), custom_call_target="tpu_custom_call" | custom-call | flops 6442450944 | bytes 3145728 | tf_op jit(solution)/shard_map/gated_ffn/pallas_call | solution.py:203
  202.5 3.7 %collective-permute-done.38 = bf16[48,2048]{1,0:T(8,128)(2,1)S(1)} collective-permute-done((bf16[48,2048]{1,0:T(8,128)(2,1)S(1)}, bf16[48,2048]{1,0:T(8,128)(2,1)S(1)}, u32[]{:S(2)}, u32[]{:S(2)}) %collective-permute-start.38) | collective-permute-done | bytes 196640 | tf_op jit(solution)/shard_map/ppermute | solution.py:161
  212.8 11.1 %collective-permute-done.42 = bf16[48,2048]{1,0:T(8,128)(2,1)S(1)} collective-permute-done((bf16[48,2048]{1,0:T(8,128)(2,1)S(1)}, bf16[48,2048]{1,0:T(8,128)(2,1)S(1)}, u32[]{:S(2)}, u32[]{:S(2)}) %collective-permute-start.42) | collective-permute-done | bytes 196640 | tf_op jit(solution)/shard_map/ppermute | solution.py:161
  227.2 6.2 %collective-permute-done.44 = bf16[96,2048]{1,0:T(8,128)(2,1)S(1)} collective-permute-done((bf16[96,2048]{1,0:T(8,128)(2,1)S(1)}, bf16[96,2048]{1,0:T(8,128)(2,1)S(1)}, u32[]{:S(2)}, u32[]{:S(2)}) %collective-permute-start.44) | collective-permute-done | bytes 393248 | tf_op jit(solution)/shard_map/ppermute | solution.py:165
  233.7 2.4 collective-permute-done.47
  (214 shorter events, 57.7 us)
Async XLA Ops:
  3.7 37.0 %all-to-all-start = ((bf16[8,96,768]{2,1,0:T(8,128)(2,1)}), bf16[8,96,768]{2,1,0:T(8,128)(2,1)S(1)}, u32[]{:S(2)}, u32[]{:S(2)}) async-start(bf16[8,96,768]{2,1,0:T(8,128)(2,1)} %pad_maximum_fusion), calls=%async_computation | async-start | bytes 2359296 | tf_op jit(solution)/shard_map/all_to_all | solution.py:148
  23.9 25.4 %collective-permute-start.16 = (f32[2,4,4,96]{3,2,1,0:T(4,128)S(1)}, f32[2,4,4,96]{3,2,1,0:T(4,128)S(1)}, u32[]{:S(2)}, u32[]{:S(2)}) collective-permute-start(f32[2,4,4,96]{3,2,1,0:T(4,128)S(1)} %pad_maximum_fusion.3), channel_id=1, source_target_pairs={{0,8},{4,12},{8,16},{12,20},{16,24},{20,28},{24,0},{28,4},{1,9},{5... | collective-permute-start | bytes 36872 | tf_op jit(solution)/shard_map/ppermute | solution.py:169
  27.5 21.9 %collective-permute-start.22 = (f32[2,4,4,96]{3,2,1,0:T(4,128)S(1)}, f32[2,4,4,96]{3,2,1,0:T(4,128)S(1)}, u32[]{:S(2)}, u32[]{:S(2)}) collective-permute-start(f32[2,4,4,96]{3,2,1,0:T(4,128)S(1)} %pad_maximum_fusion.3), channel_id=1, source_target_pairs={{0,16},{4,20},{8,24},{12,28},{16,0},{20,4},{24,8},{28,12},{1,17},{... | collective-permute-start | bytes 36872 | tf_op jit(solution)/shard_map/ppermute | solution.py:169
  29.5 34.8 %collective-permute-start.30 = (f32[2,4,4,96]{3,2,1,0:T(4,128)S(1)}, f32[2,4,4,96]{3,2,1,0:T(4,128)S(1)}, u32[]{:S(2)}, u32[]{:S(2)}) collective-permute-start(f32[2,4,4,96]{3,2,1,0:T(4,128)S(1)} %pad_maximum_fusion.3), channel_id=1, source_target_pairs={{0,24},{4,28},{8,0},{12,4},{16,8},{20,12},{24,16},{28,20},{1,25},{... | collective-permute-start | bytes 36872 | tf_op jit(solution)/shard_map/ppermute | solution.py:169
  45.6 15.1 %all-to-all-start.1 = ((bf16[8,96,256]{2,1,0:T(8,128)(2,1)}), bf16[8,96,256]{2,1,0:T(8,128)(2,1)S(1)}, u32[]{:S(2)}, u32[]{:S(2)}) async-start(bf16[8,96,256]{2,1,0:T(8,128)(2,1)} %bitcast.5), calls=%async_computation.1 | async-start | bytes 786432 | tf_op jit(solution)/shard_map/all_to_all | solution.py:150
  64.3 11.3 %collective-permute-start.2 = (bf16[96,2048]{1,0:T(8,128)(2,1)S(1)}, bf16[96,2048]{1,0:T(8,128)(2,1)S(1)}, u32[]{:S(2)}, u32[]{:S(2)}) collective-permute-start(bf16[96,2048]{1,0:T(8,128)(2,1)S(1)} %fusion.1), channel_id=1, source_target_pairs={{0,8},{4,12},{8,16},{12,20},{16,24},{20,28},{24,0},{28,4},{1,9},{5... | collective-permute-start | bytes 1179656 | tf_op jit(solution)/shard_map/ppermute | solution.py:169
  78.0 21.9 %collective-permute-start.6 = (bf16[96,2048]{1,0:T(8,128)(2,1)S(1)}, bf16[96,2048]{1,0:T(8,128)(2,1)S(1)}, u32[]{:S(2)}, u32[]{:S(2)}) collective-permute-start(bf16[96,2048]{1,0:T(8,128)(2,1)S(1)} %collective-permute-done.2), channel_id=1, source_target_pairs={{0,4},{4,0},{8,12},{12,8},{16,20},{20,16},{24,28},{28,24},{1,5},{5... | collective-permute-start | bytes 1179656 | tf_op jit(solution)/shard_map/ppermute | solution.py:165
  79.7 20.2 %collective-permute-start.7 = (bf16[96,2048]{1,0:T(8,128)(2,1)S(1)}, bf16[96,2048]{1,0:T(8,128)(2,1)S(1)}, u32[]{:S(2)}, u32[]{:S(2)}) collective-permute-start(bf16[96,2048]{1,0:T(8,128)(2,1)S(1)} %collective-permute-done.2), channel_id=1, source_target_pairs={{0,2},{1,3},{2,0},{3,1},{4,6},{5,7},{6,4},{7,5},{8,10},{9,11},{10,... | collective-permute-start | bytes 1179656 | tf_op jit(solution)/shard_map/ppermute | solution.py:161
  81.2 18.7 %collective-permute-start.10 = (bf16[96,2048]{1,0:T(8,128)(2,1)S(1)}, bf16[96,2048]{1,0:T(8,128)(2,1)S(1)}, u32[]{:S(2)}, u32[]{:S(2)}) collective-permute-start(bf16[96,2048]{1,0:T(8,128)(2,1)S(1)} %collective-permute-done.2), channel_id=1, source_target_pairs={{0,8},{4,12},{8,16},{12,20},{16,24},{20,28},{24,0},{28,4},{1,9},{5... | collective-permute-start | bytes 1179656 | tf_op jit(solution)/shard_map/ppermute | solution.py:169
  110.0 13.6 %collective-permute-start.14 = (bf16[384,2048]{1,0:T(8,128)(2,1)S(1)}, bf16[384,2048]{1,0:T(8,128)(2,1)S(1)}, u32[]{:S(2)}, u32[]{:S(2)}) collective-permute-start(bf16[384,2048]{1,0:T(8,128)(2,1)S(1)} %constant_dynamic-update-slice_fusion.5.rows_ref), channel_id=1, source_target_pairs={{0,1},{1,0},{2,3},{3,2},{4,5},{5,4},{6,7},{7,6},{8,9},{9,8},{10,11... | collective-permute-start | bytes 4718600 | tf_op jit(solution)/shard_map/ppermute | solution.py:157
  110.1 13.5 %collective-permute-start.17 = (bf16[96,2048]{1,0:T(8,128)(2,1)S(1)}, bf16[96,2048]{1,0:T(8,128)(2,1)S(1)}, u32[]{:S(2)}, u32[]{:S(2)}) collective-permute-start(bf16[96,2048]{1,0:T(8,128)(2,1)S(1)} %collective-permute-done.10), channel_id=1, source_target_pairs={{0,8},{4,12},{8,16},{12,20},{16,24},{20,28},{24,0},{28,4},{1,9},{5... | collective-permute-start | bytes 1179656 | tf_op jit(solution)/shard_map/ppermute | solution.py:169
  110.4 22.3 %collective-permute-start.18 = (bf16[192,2048]{1,0:T(8,128)(2,1)S(1)}, bf16[192,2048]{1,0:T(8,128)(2,1)S(1)}, u32[]{:S(2)}, u32[]{:S(2)}) collective-permute-start(bf16[192,2048]{1,0:T(8,128)(2,1)S(1)} %pad_maximum_fusion.1), channel_id=1, source_target_pairs={{0,2},{1,3},{2,0},{3,1},{4,6},{5,7},{6,4},{7,5},{8,10},{9,11},{10,... | collective-permute-start | bytes 2359304 | tf_op jit(solution)/shard_map/ppermute | solution.py:161
  134.4 11.9 %collective-permute-start.20 = (bf16[384,2048]{1,0:T(8,128)(2,1)S(1)}, bf16[384,2048]{1,0:T(8,128)(2,1)S(1)}, u32[]{:S(2)}, u32[]{:S(2)}) collective-permute-start(bf16[384,2048]{1,0:T(8,128)(2,1)S(1)} %gated_ffn.10), channel_id=1, source_target_pairs={{0,1},{1,0},{2,3},{3,2},{4,5},{5,4},{6,7},{7,6},{8,9},{9,8},{10,11... | collective-permute-start | bytes 4718600 | tf_op jit(solution)/shard_map/ppermute | solution.py:157
  134.5 11.8 %collective-permute-start.21 = (bf16[384,2048]{1,0:T(8,128)(2,1)S(1)}, bf16[384,2048]{1,0:T(8,128)(2,1)S(1)}, u32[]{:S(2)}, u32[]{:S(2)}) collective-permute-start(bf16[384,2048]{1,0:T(8,128)(2,1)S(1)} %constant_dynamic-update-slice_fusion.10.rows_ref), channel_id=1, source_target_pairs={{0,1},{1,0},{2,3},{3,2},{4,5},{5,4},{6,7},{7,6},{8,9},{9,8},{10,11... | collective-permute-start | bytes 4718600 | tf_op jit(solution)/shard_map/ppermute | solution.py:157
  136.0 20.8 %collective-permute-start.25 = (bf16[192,2048]{1,0:T(8,128)(2,1)}, bf16[192,2048]{1,0:T(8,128)(2,1)S(1)}, u32[]{:S(2)}, u32[]{:S(2)}) collective-permute-start(bf16[192,2048]{1,0:T(8,128)(2,1)} %pad_maximum_fusion.2), channel_id=1, source_target_pairs={{0,2},{1,3},{2,0},{3,1},{4,6},{5,7},{6,4},{7,5},{8,10},{9,11},{10,... | collective-permute-start | bytes 2359304 | tf_op jit(solution)/shard_map/ppermute | solution.py:161
  147.0 13.0 %collective-permute-start.23 = (bf16[48,2048]{1,0:T(8,128)(2,1)S(1)}, bf16[48,2048]{1,0:T(8,128)(2,1)S(1)}, u32[]{:S(2)}, u32[]{:S(2)}) collective-permute-start(bf16[48,2048]{1,0:T(8,128)(2,1)S(1)} %get-tuple-element.304), channel_id=1, source_target_pairs={{0,2},{1,3},{2,0},{3,1},{4,6},{5,7},{6,4},{7,5},{8,10},{9,11},{10,... | collective-permute-start | bytes 589832 | tf_op jit(solution)/shard_map/ppermute | solution.py:161
  147.6 12.4 %collective-permute-start.24 = (bf16[48,2048]{1,0:T(8,128)(2,1)S(1)}, bf16[48,2048]{1,0:T(8,128)(2,1)S(1)}, u32[]{:S(2)}, u32[]{:S(2)}) collective-permute-start(bf16[48,2048]{1,0:T(8,128)(2,1)S(1)} %get-tuple-element.303), channel_id=1, source_target_pairs={{0,4},{4,0},{8,12},{12,8},{16,20},{20,16},{24,28},{28,24},{1,5},{5... | collective-permute-start | bytes 589832 | tf_op jit(solution)/shard_map/ppermute | solution.py:165
  160.0 12.8 %collective-permute-start.26 = (bf16[384,2048]{1,0:T(8,128)(2,1)S(1)}, bf16[384,2048]{1,0:T(8,128)(2,1)S(1)}, u32[]{:S(2)}, u32[]{:S(2)}) collective-permute-start(bf16[384,2048]{1,0:T(8,128)(2,1)S(1)} %gated_ffn.12), channel_id=1, source_target_pairs={{0,1},{1,0},{2,3},{3,2},{4,5},{5,4},{6,7},{7,6},{8,9},{9,8},{10,11... | collective-permute-start | bytes 4718600 | tf_op jit(solution)/shard_map/ppermute | solution.py:157
  160.1 12.6 %collective-permute-start.29 = (bf16[384,2048]{1,0:T(8,128)(2,1)S(1)}, bf16[384,2048]{1,0:T(8,128)(2,1)S(1)}, u32[]{:S(2)}, u32[]{:S(2)}) collective-permute-start(bf16[384,2048]{1,0:T(8,128)(2,1)S(1)} %constant_dynamic-update-slice_fusion.13.rows_ref), channel_id=1, source_target_pairs={{0,1},{1,0},{2,3},{3,2},{4,5},{5,4},{6,7},{7,6},{8,9},{9,8},{10,11... | collective-permute-start | bytes 4718600 | tf_op jit(solution)/shard_map/ppermute | solution.py:157
  160.7 25.0 %collective-permute-start.5 = (bf16[384,2048]{1,0:T(8,128)(2,1)S(1)}, bf16[384,2048]{1,0:T(8,128)(2,1)S(1)}, u32[]{:S(2)}, u32[]{:S(2)}) collective-permute-start(bf16[384,2048]{1,0:T(8,128)(2,1)S(1)} %constant_dynamic-update-slice_fusion.rows_ref), channel_id=1, source_target_pairs={{0,1},{1,0},{2,3},{3,2},{4,5},{5,4},{6,7},{7,6},{8,9},{9,8},{10,11... | collective-permute-start | bytes 4718600 | tf_op jit(solution)/shard_map/ppermute | solution.py:157
  160.9 11.6 %collective-permute-start.27 = (bf16[96,2048]{1,0:T(8,128)(2,1)S(1)}, bf16[96,2048]{1,0:T(8,128)(2,1)S(1)}, u32[]{:S(2)}, u32[]{:S(2)}) collective-permute-start(bf16[96,2048]{1,0:T(8,128)(2,1)S(1)} %convert_element_type.181), channel_id=1, source_target_pairs={{0,4},{4,0},{8,12},{12,8},{16,20},{20,16},{24,28},{28,24},{1,5},{5... | collective-permute-start | bytes 1179656 | tf_op jit(solution)/shard_map/ppermute | solution.py:165
  161.4 11.3 %collective-permute-start.28 = (bf16[96,2048]{1,0:T(8,128)(2,1)S(1)}, bf16[96,2048]{1,0:T(8,128)(2,1)S(1)}, u32[]{:S(2)}, u32[]{:S(2)}) collective-permute-start(bf16[96,2048]{1,0:T(8,128)(2,1)S(1)} %convert_element_type.183), channel_id=1, source_target_pairs={{0,2},{1,3},{2,0},{3,1},{4,6},{5,7},{6,4},{7,5},{8,10},{9,11},{10,... | collective-permute-start | bytes 1179656 | tf_op jit(solution)/shard_map/ppermute | solution.py:161
  173.4 12.2 %collective-permute-start.31 = (bf16[48,2048]{1,0:T(8,128)(2,1)S(1)}, bf16[48,2048]{1,0:T(8,128)(2,1)S(1)}, u32[]{:S(2)}, u32[]{:S(2)}) collective-permute-start(bf16[48,2048]{1,0:T(8,128)(2,1)S(1)} %get-tuple-element.302), channel_id=1, source_target_pairs={{0,2},{1,3},{2,0},{3,1},{4,6},{5,7},{6,4},{7,5},{8,10},{9,11},{10,... | collective-permute-start | bytes 589832 | tf_op jit(solution)/shard_map/ppermute | solution.py:161
  185.7 12.5 %collective-permute-start.33 = (bf16[384,2048]{1,0:T(8,128)(2,1)S(1)}, bf16[384,2048]{1,0:T(8,128)(2,1)S(1)}, u32[]{:S(2)}, u32[]{:S(2)}) collective-permute-start(bf16[384,2048]{1,0:T(8,128)(2,1)S(1)} %gated_ffn.14), channel_id=1, source_target_pairs={{0,1},{1,0},{2,3},{3,2},{4,5},{5,4},{6,7},{7,6},{8,9},{9,8},{10,11... | collective-permute-start | bytes 4718600 | tf_op jit(solution)/shard_map/ppermute | solution.py:157
  185.9 11.8 %collective-permute-start.36 = (bf16[96,2048]{1,0:T(8,128)(2,1)S(1)}, bf16[96,2048]{1,0:T(8,128)(2,1)S(1)}, u32[]{:S(2)}, u32[]{:S(2)}) collective-permute-start(bf16[96,2048]{1,0:T(8,128)(2,1)S(1)} %add_convert_fusion.2), channel_id=1, source_target_pairs={{0,24},{4,28},{8,0},{12,4},{16,8},{20,12},{24,16},{28,20},{1,25},{... | collective-permute-start | bytes 1179656 | tf_op jit(solution)/shard_map/ppermute | solution.py:169
  186.6 11.3 %collective-permute-start.34 = (bf16[96,2048]{1,0:T(8,128)(2,1)S(1)}, bf16[96,2048]{1,0:T(8,128)(2,1)S(1)}, u32[]{:S(2)}, u32[]{:S(2)}) collective-permute-start(bf16[96,2048]{1,0:T(8,128)(2,1)S(1)} %convert_element_type.187), channel_id=1, source_target_pairs={{0,4},{4,0},{8,12},{12,8},{16,20},{20,16},{24,28},{28,24},{1,5},{5... | collective-permute-start | bytes 1179656 | tf_op jit(solution)/shard_map/ppermute | solution.py:165
  187.1 11.0 %collective-permute-start.35 = (bf16[96,2048]{1,0:T(8,128)(2,1)S(1)}, bf16[96,2048]{1,0:T(8,128)(2,1)S(1)}, u32[]{:S(2)}, u32[]{:S(2)}) collective-permute-start(bf16[96,2048]{1,0:T(8,128)(2,1)S(1)} %convert_element_type.189), channel_id=1, source_target_pairs={{0,2},{1,3},{2,0},{3,1},{4,6},{5,7},{6,4},{7,5},{8,10},{9,11},{10,... | collective-permute-start | bytes 1179656 | tf_op jit(solution)/shard_map/ppermute | solution.py:161
  202.4 24.8 %collective-permute-start.46 = (bf16[96,2048]{1,0:T(8,128)(2,1)S(1)}, bf16[96,2048]{1,0:T(8,128)(2,1)S(1)}, u32[]{:S(2)}, u32[]{:S(2)}) collective-permute-start(bf16[96,2048]{1,0:T(8,128)(2,1)S(1)} %add_convert_fusion.1), channel_id=1, source_target_pairs={{0,16},{4,20},{8,24},{12,28},{16,0},{20,4},{24,8},{28,12},{1,17},{... | collective-permute-start | bytes 1179656 | tf_op jit(solution)/shard_map/ppermute | solution.py:169
  207.6 16.4 %collective-permute-start.40 = (bf16[96,2048]{1,0:T(8,128)(2,1)S(1)}, bf16[96,2048]{1,0:T(8,128)(2,1)S(1)}, u32[]{:S(2)}, u32[]{:S(2)}) collective-permute-start(bf16[96,2048]{1,0:T(8,128)(2,1)S(1)} %convert_element_type.196), channel_id=1, source_target_pairs={{0,4},{4,0},{8,12},{12,8},{16,20},{20,16},{24,28},{28,24},{1,5},{5... | collective-permute-start | bytes 1179656 | tf_op jit(solution)/shard_map/ppermute | solution.py:165
  209.5 14.4 %collective-permute-start.41 = (bf16[96,2048]{1,0:T(8,128)(2,1)S(1)}, bf16[96,2048]{1,0:T(8,128)(2,1)S(1)}, u32[]{:S(2)}, u32[]{:S(2)}) collective-permute-start(bf16[96,2048]{1,0:T(8,128)(2,1)S(1)} %convert_element_type.198), channel_id=1, source_target_pairs={{0,2},{1,3},{2,0},{3,1},{4,6},{5,7},{6,4},{7,5},{8,10},{9,11},{10,... | collective-permute-start | bytes 1179656 | tf_op jit(solution)/shard_map/ppermute | solution.py:161
  210.8 13.1 %collective-permute-start.42 = (bf16[48,2048]{1,0:T(8,128)(2,1)S(1)}, bf16[48,2048]{1,0:T(8,128)(2,1)S(1)}, u32[]{:S(2)}, u32[]{:S(2)}) collective-permute-start(bf16[48,2048]{1,0:T(8,128)(2,1)S(1)} %get-tuple-element.298), channel_id=1, source_target_pairs={{0,2},{1,3},{2,0},{3,1},{4,6},{5,7},{6,4},{7,5},{8,10},{9,11},{10,... | collective-permute-start | bytes 589832 | tf_op jit(solution)/shard_map/ppermute | solution.py:161
  212.4 11.6 %collective-permute-start.43 = (bf16[48,2048]{1,0:T(8,128)(2,1)S(1)}, bf16[48,2048]{1,0:T(8,128)(2,1)S(1)}, u32[]{:S(2)}, u32[]{:S(2)}) collective-permute-start(bf16[48,2048]{1,0:T(8,128)(2,1)S(1)} %get-tuple-element.297), channel_id=1, source_target_pairs={{0,4},{4,0},{8,12},{12,8},{16,20},{20,16},{24,28},{28,24},{1,5},{5... | collective-permute-start | bytes 589832 | tf_op jit(solution)/shard_map/ppermute | solution.py:165
  (26 other events, 206.2 us)
where the time goes:
time: 238 us; the launch traced here: 237 us
  waiting for transfers between devices  84.7 us (36%)
  Pallas kernels  74.8 us (31%)
  starting transfers between devices  56.6 us (24%)
  local copies, waits for them, and re-layouts  12.1 us (5%)
  other arithmetic  8.02 us (3%)
    pallas_call x8, Pallas kernels, gated_ffn(): pl.pallas_call(ffn_kernel, in_specs=[vmem] * 4, out_specs=vmem, out_shape...  69.9 us
    ppermute x15, waiting for transfers between devices, swap_y(): return lax.ppermute(a, 'ctx', [(i, i ^ 1) for i in range(8)])  27.3 us
    ppermute x15, waiting for transfers between devices, swap_x(): return lax.ppermute(a, 'exp', [(i, i ^ 2) for i in range(4)])  27 us
    ppermute x15, starting transfers between devices, swap_x(): return lax.ppermute(a, 'exp', [(i, i ^ 2) for i in range(4)])  19.3 us
    ppermute x15, starting transfers between devices, swap_y(): return lax.ppermute(a, 'ctx', [(i, i ^ 1) for i in range(8)])  15.1 us
    all_to_all x1, waiting for transfers between devices, attention(): lax.all_to_all(mixed.reshape(n_ctx, tok_count, piece), 'ctx', split_axis=...  11.4 us
    ppermute x9, starting transfers between devices, turn_z(): return lax.ppermute(a, 'ctx', [(i, (i + 2 * steps) % 8) for i in range(8)])  9.97 us
    all_to_all x1, waiting for transfers between devices, attention(): lax.all_to_all(outgoing, 'ctx', split_axis=0, concat_axis=0, tiled=True)  9.45 us
  transfers between devices with their start and end apart: 50, of which 26 were waited for; matrix products, arithmetic and copies ran while one was open for 4% of the time, Pallas kernels for 32%

commit v1 on v0

--- a/solution.py
+++ b/solution.py
@@ -171,7 +171,7 @@
 
 def ffn_kernel(rows_ref, gate_ref, first_ref, second_ref, out_ref, act_ref):
     n_exp, width, inner = first_ref.shape
-    cut = 512
+    cut = 1024
     per = inner // cut
     gates = gate_ref[...].T
 

time: 238 us -> 236 us (level)
  Pallas kernels: 74.8 us -> 69.6 us
  waiting for transfers between devices: 84.7 us -> 89.1 us
    pallas_call x8, Pallas kernels: 69.9 us -> 64.7 us  [gated_ffn(): pl.pallas_call(ffn_kernel, in_specs=[vmem] * 4, out_specs=vmem, out_shape...]
  transfers between devices with their start and end apart: 50 -> 50, of which waited for: 26 -> 27; matrix products, arithmetic and copies ran while one was open for 4% -> 4% of each run, Pallas kernels for 32% -> 30%
where the time goes in v1:
time: 236 us; the launch traced here: 235 us
  waiting for transfers between devices  89.1 us (38%)
  Pallas kernels  69.6 us (29%)
  starting transfers between devices  55.8 us (24%)
  local copies, waits for them, and re-layouts  12.1 us (5%)
  other arithmetic  8.03 us (3%)
    pallas_call x8, Pallas kernels, gated_ffn(): pl.pallas_call(ffn_kernel, in_specs=[vmem] * 4, out_specs=vmem, out_shape...  64.7 us
    ppermute x15, waiting for transfers between devices, swap_x(): return lax.ppermute(a, 'exp', [(i, i ^ 2) for i in range(4)])  28.8 us
    ppermute x15, waiting for transfers between devices, swap_y(): return lax.ppermute(a, 'ctx', [(i, i ^ 1) for i in range(8)])  27.5 us
    ppermute x15, starting transfers between devices, swap_x(): return lax.ppermute(a, 'exp', [(i, i ^ 2) for i in range(4)])  18.9 us
    ppermute x15, starting transfers between devices, swap_y(): return lax.ppermute(a, 'ctx', [(i, i ^ 1) for i in range(8)])  15.1 us
    all_to_all x1, waiting for transfers between devices, attention(): lax.all_to_all(mixed.reshape(n_ctx, tok_count, piece), 'ctx', split_axis=...  11.4 us
    ppermute x9, waiting for transfers between devices, turn_z(): return lax.ppermute(a, 'ctx', [(i, (i + 2 * steps) % 8) for i in range(8)])  10.9 us
    ppermute x9, starting transfers between devices, turn_z(): return lax.ppermute(a, 'ctx', [(i, (i + 2 * steps) % 8) for i in range(8)])  9.52 us
  transfers between devices with their start and end apart: 50, of which 27 were waited for; matrix products, arithmetic and copies ran while one was open for 4% of the time, Pallas kernels for 30%

profile of v1, /device:TPU:0, one launch (start us, length us, event | category | flops | bytes accessed | tf_op | source)
XLA Modules:
  0.0 235.5 jit_solution(8387406732941224458)
XLA Ops:
  3.7 7.4 %all-to-all-start = ((bf16[8,96,768]{2,1,0:T(8,128)(2,1)}), bf16[8,96,768]{2,1,0:T(8,128)(2,1)S(1)}, u32[]{:S(2)}, u32[]{:S(2)}) async-start(bf16[8,96,768]{2,1,0:T(8,128)(2,1)} %pad_maximum_fusion), calls=%async_computation | async-start | bytes 2359296 | tf_op jit(solution)/shard_map/all_to_all | solution.py:148
  11.2 2.1 collective-permute-start.8
  13.2 5.9 %collective-permute-done.8 = f32[4,96]{1,0:T(4,128)S(1)} collective-permute-done((f32[4,96]{1,0:T(4,128)S(1)}, f32[4,96]{1,0:T(4,128)S(1)}, u32[]{:S(2)}, u32[]{:S(2)}) %collective-permute-start.8) | collective-permute-done | bytes 1568 | tf_op jit(solution)/shard_map/ppermute | solution.py:165
  20.6 2.1 collective-permute-done.9
  23.9 3.5 %collective-permute-start.16 = (f32[2,4,4,96]{3,2,1,0:T(4,128)S(1)}, f32[2,4,4,96]{3,2,1,0:T(4,128)S(1)}, u32[]{:S(2)}, u32[]{:S(2)}) collective-permute-start(f32[2,4,4,96]{3,2,1,0:T(4,128)S(1)} %pad_maximum_fusion.3), channel_id=1, source_target_pairs={{0,8},{4,12},{8,16},{12,20},{16,24},{20,28},{24,0},{28,4},{1,9},{5... | collective-permute-start | bytes 36872 | tf_op jit(solution)/shard_map/ppermute | solution.py:169
  27.5 2.1 collective-permute-start.22
  31.3 9.4 %all-to-all-done = bf16[8,96,768]{2,1,0:T(8,128)(2,1)S(1)} async-done(((bf16[8,96,768]{2,1,0:T(8,128)(2,1)}), bf16[8,96,768]{2,1,0:T(8,128)(2,1)S(1)}, u32[]{:S(2)}, u32[]{:S(2)}) %all-to-all-start) | async-done | bytes 1179680 | tf_op jit(solution)/shard_map/all_to_all | solution.py:148
  40.7 4.9 %attend_heads.1 = bf16[768,256]{1,0:T(8,128)(2,1)} custom-call(bf16[768,768]{1,0:T(8,128)(2,1)S(1)} %bitcast.86, bf16[768,768]{1,0:T(8,128)(2,1)S(1)} %bitcast.87, bf16[768,768]{1,0:T(8,128)(2,1)S(1)} %bitcast.88), custom_call_target="tpu_custom_call" | custom-call | flops 603979776 | bytes 1572864 | tf_op jit(solution)/shard_map/attend_heads/pallas_call | solution.py:119
  45.6 3.5 %all-to-all-start.1 = ((bf16[8,96,256]{2,1,0:T(8,128)(2,1)}), bf16[8,96,256]{2,1,0:T(8,128)(2,1)S(1)}, u32[]{:S(2)}, u32[]{:S(2)}) async-start(bf16[8,96,256]{2,1,0:T(8,128)(2,1)} %bitcast.5), calls=%async_computation.1 | async-start | bytes 786432 | tf_op jit(solution)/shard_map/all_to_all | solution.py:150
  49.4 11.4 %all-to-all-done.1 = bf16[8,96,256]{2,1,0:T(8,128)(2,1)S(1)} async-done(((bf16[8,96,256]{2,1,0:T(8,128)(2,1)}), bf16[8,96,256]{2,1,0:T(8,128)(2,1)S(1)}, u32[]{:S(2)}, u32[]{:S(2)}) %all-to-all-start.1) | async-done | bytes 393248 | tf_op jit(solution)/shard_map/all_to_all | solution.py:150
  64.3 6.8 %collective-permute-done = bf16[96,2048]{1,0:T(8,128)(2,1)S(1)} collective-permute-done((bf16[96,2048]{1,0:T(8,128)(2,1)S(1)}, bf16[96,2048]{1,0:T(8,128)(2,1)S(1)}, u32[]{:S(2)}, u32[]{:S(2)}) %collective-permute-start) | collective-permute-done | bytes 393248 | tf_op jit(solution)/shard_map/ppermute | solution.py:165
  72.6 3.0 %collective-permute-done.2 = bf16[96,2048]{1,0:T(8,128)(2,1)S(1)} collective-permute-done((bf16[96,2048]{1,0:T(8,128)(2,1)S(1)}, bf16[96,2048]{1,0:T(8,128)(2,1)S(1)}, u32[]{:S(2)}, u32[]{:S(2)}) %collective-permute-start.2) | collective-permute-done | bytes 393248 | tf_op jit(solution)/shard_map/ppermute | solution.py:169
  81.2 2.3 collective-permute-done.3
  84.3 3.4 %copy-done = bf16[2,2048,1024]{2,1,0:T(8,128)(2,1)S(1)} copy-done((bf16[2,2048,1024]{2,1,0:T(8,128)(2,1)S(1)}, bf16[2,2048,1024]{2,1,0:T(8,128)(2,1)}, u32[]{:S(2)}) %copy-start) | copy-done | bytes 8388632
  87.7 3.4 %copy-done.1 = bf16[2,1024,2048]{2,1,0:T(8,128)(2,1)S(1)} copy-done((bf16[2,1024,2048]{2,1,0:T(8,128)(2,1)S(1)}, bf16[2,1024,2048]{2,1,0:T(8,128)(2,1)}, u32[]{:S(2)}) %copy-start.1) | copy-done | bytes 8388632
  91.1 8.0 %gated_ffn.8 = bf16[384,2048]{1,0:T(8,128)(2,1)S(1)} custom-call(bf16[384,2048]{1,0:T(8,128)(2,1)S(1)} %constant_dynamic-update-slice_fusion.rows_ref, f32[8,384]{1,0:T(8,128)S(1)} %pad.41.gate_ref, bf16[2,2048,1024]{2,1,0:T(8,128)(2,1)S(1)} %copy-done, bf16[2048,2048]{1,0:T(8,128)(2,1)S(1)} %bitcast.91), custom_call_target="tpu_custom_call" | custom-call | flops 6442450944 | bytes 3145728 | tf_op jit(solution)/shard_map/gated_ffn/pallas_call | solution.py:203
  102.9 2.4 %collective-permute-done.11 = bf16[48,2048]{1,0:T(8,128)(2,1)S(1)} collective-permute-done((bf16[48,2048]{1,0:T(8,128)(2,1)S(1)}, bf16[48,2048]{1,0:T(8,128)(2,1)S(1)}, u32[]{:S(2)}, u32[]{:S(2)}) %collective-permute-start.11) | collective-permute-done | bytes 196640 | tf_op jit(solution)/shard_map/ppermute | solution.py:161
  105.3 3.8 %collective-permute-done.12 = bf16[48,2048]{1,0:T(8,128)(2,1)S(1)} collective-permute-done((bf16[48,2048]{1,0:T(8,128)(2,1)S(1)}, bf16[48,2048]{1,0:T(8,128)(2,1)S(1)}, u32[]{:S(2)}, u32[]{:S(2)}) %collective-permute-start.12) | collective-permute-done | bytes 196640 | tf_op jit(solution)/shard_map/ppermute | solution.py:165
  111.2 8.0 %gated_ffn.9 = bf16[384,2048]{1,0:T(8,128)(2,1)S(1)} custom-call(bf16[384,2048]{1,0:T(8,128)(2,1)S(1)} %constant_dynamic-update-slice_fusion.5.rows_ref, f32[8,384]{1,0:T(8,128)S(1)} %pad.42.gate_ref, bf16[2,2048,1024]{2,1,0:T(8,128)(2,1)S(1)} %copy-done, bf16[2048,2048]{1,0:T(8,128)(2,1)S(1)} %bitcast.92), custom_call_target="tpu_custom_call" | custom-call | flops 6442450944 | bytes 3145728 | tf_op jit(solution)/shard_map/gated_ffn/pallas_call | solution.py:203
  119.3 3.6 %collective-permute-done.17 = bf16[96,2048]{1,0:T(8,128)(2,1)S(1)} collective-permute-done((bf16[96,2048]{1,0:T(8,128)(2,1)S(1)}, bf16[96,2048]{1,0:T(8,128)(2,1)S(1)}, u32[]{:S(2)}, u32[]{:S(2)}) %collective-permute-start.17) | collective-permute-done | bytes 393248 | tf_op jit(solution)/shard_map/ppermute | solution.py:169
  123.2 8.0 %gated_ffn.10 = bf16[384,2048]{1,0:T(8,128)(2,1)S(1)} custom-call(bf16[384,2048]{1,0:T(8,128)(2,1)S(1)} %collective-permute-done.14.rows_ref, f32[8,384]{1,0:T(8,128)S(1)} %pad.43.gate_ref, bf16[2,2048,1024]{2,1,0:T(8,128)(2,1)S(1)} %copy-done, bf16[2048,2048]{1,0:T(8,128)(2,1)S(1)} %bitcast.93), custom_call_target="tpu_custom_call" | custom-call | flops 6442450944 | bytes 3145728 | tf_op jit(solution)/shard_map/gated_ffn/pallas_call | solution.py:203
  131.2 2.4 %collective-permute-done.19 = bf16[96,2048]{1,0:T(8,128)(2,1)S(1)} collective-permute-done((bf16[96,2048]{1,0:T(8,128)(2,1)S(1)}, bf16[96,2048]{1,0:T(8,128)(2,1)S(1)}, u32[]{:S(2)}, u32[]{:S(2)}) %collective-permute-start.19) | collective-permute-done | bytes 393248 | tf_op jit(solution)/shard_map/ppermute | solution.py:165
  136.8 8.0 %gated_ffn.11 = bf16[384,2048]{1,0:T(8,128)(2,1)S(1)} custom-call(bf16[384,2048]{1,0:T(8,128)(2,1)S(1)} %constant_dynamic-update-slice_fusion.10.rows_ref, f32[8,384]{1,0:T(8,128)S(1)} %pad.44.gate_ref, bf16[2,2048,1024]{2,1,0:T(8,128)(2,1)S(1)} %copy-done, bf16[2048,2048]{1,0:T(8,128)(2,1)S(1)} %bitcast.94), custom_call_target="tpu_custom_call" | custom-call | flops 6442450944 | bytes 3145728 | tf_op jit(solution)/shard_map/gated_ffn/pallas_call | solution.py:203
  146.4 8.2 %gated_ffn.12 = bf16[384,2048]{1,0:T(8,128)(2,1)S(1)} custom-call(bf16[384,2048]{1,0:T(8,128)(2,1)S(1)} %collective-permute-done.21.rows_ref, f32[8,384]{1,0:T(8,128)S(1)} %pad.45.gate_ref, bf16[2,2048,1024]{2,1,0:T(8,128)(2,1)S(1)} %bitcast.90, bf16[2048,2048]{1,0:T(8,128)(2,1)S(1)} %bitcast.95), custom_call_target="tpu_custom_call" | custom-call | flops 6442450944 | bytes 3145728 | tf_op jit(solution)/shard_map/gated_ffn/pallas_call | solution.py:203
  155.9 3.3 %collective-permute-done.23 = bf16[48,2048]{1,0:T(8,128)(2,1)S(1)} collective-permute-done((bf16[48,2048]{1,0:T(8,128)(2,1)S(1)}, bf16[48,2048]{1,0:T(8,128)(2,1)S(1)}, u32[]{:S(2)}, u32[]{:S(2)}) %collective-permute-start.23) | collective-permute-done | bytes 196640 | tf_op jit(solution)/shard_map/ppermute | solution.py:161
  162.3 8.0 %gated_ffn.13 = bf16[384,2048]{1,0:T(8,128)(2,1)S(1)} custom-call(bf16[384,2048]{1,0:T(8,128)(2,1)S(1)} %constant_dynamic-update-slice_fusion.13.rows_ref, f32[8,384]{1,0:T(8,128)S(1)} %pad.46.gate_ref, bf16[2,2048,1024]{2,1,0:T(8,128)(2,1)S(1)} %bitcast.90, bf16[2048,2048]{1,0:T(8,128)(2,1)S(1)} %bitcast.96), custom_call_target="tpu_custom_call" | custom-call | flops 6442450944 | bytes 3145728 | tf_op jit(solution)/shard_map/gated_ffn/pallas_call | solution.py:203
  176.0 8.0 %gated_ffn.14 = bf16[384,2048]{1,0:T(8,128)(2,1)S(1)} custom-call(bf16[384,2048]{1,0:T(8,128)(2,1)S(1)} %collective-permute-done.29.rows_ref, f32[8,384]{1,0:T(8,128)S(1)} %pad.47.gate_ref, bf16[2,2048,1024]{2,1,0:T(8,128)(2,1)S(1)} %bitcast.90, bf16[2048,2048]{1,0:T(8,128)(2,1)S(1)} %bitcast.97), custom_call_target="tpu_custom_call" | custom-call | flops 6442450944 | bytes 3145728 | tf_op jit(solution)/shard_map/gated_ffn/pallas_call | solution.py:203
  186.4 8.3 %gated_ffn.15 = bf16[384,2048]{1,0:T(8,128)(2,1)S(1)} custom-call(bf16[384,2048]{1,0:T(8,128)(2,1)S(1)} %collective-permute-done.5.rows_ref, f32[8,384]{1,0:T(8,128)S(1)} %pad.48.gate_ref, bf16[2,2048,1024]{2,1,0:T(8,128)(2,1)S(1)} %bitcast.90, bf16[2048,2048]{1,0:T(8,128)(2,1)S(1)} %bitcast.98), custom_call_target="tpu_custom_call" | custom-call | flops 6442450944 | bytes 3145728 | tf_op jit(solution)/shard_map/gated_ffn/pallas_call | solution.py:203
  200.2 4.4 %collective-permute-done.38 = bf16[48,2048]{1,0:T(8,128)(2,1)S(1)} collective-permute-done((bf16[48,2048]{1,0:T(8,128)(2,1)S(1)}, bf16[48,2048]{1,0:T(8,128)(2,1)S(1)}, u32[]{:S(2)}, u32[]{:S(2)}) %collective-permute-start.38) | collective-permute-done | bytes 196640 | tf_op jit(solution)/shard_map/ppermute | solution.py:161
  210.6 11.1 %collective-permute-done.42 = bf16[48,2048]{1,0:T(8,128)(2,1)S(1)} collective-permute-done((bf16[48,2048]{1,0:T(8,128)(2,1)S(1)}, bf16[48,2048]{1,0:T(8,128)(2,1)S(1)}, u32[]{:S(2)}, u32[]{:S(2)}) %collective-permute-start.42) | collective-permute-done | bytes 196640 | tf_op jit(solution)/shard_map/ppermute | solution.py:161
  225.5 5.5 %collective-permute-done.44 = bf16[96,2048]{1,0:T(8,128)(2,1)S(1)} collective-permute-done((bf16[96,2048]{1,0:T(8,128)(2,1)S(1)}, bf16[96,2048]{1,0:T(8,128)(2,1)S(1)}, u32[]{:S(2)}, u32[]{:S(2)}) %collective-permute-start.44) | collective-permute-done | bytes 393248 | tf_op jit(solution)/shard_map/ppermute | solution.py:165
  231.4 2.9 %collective-permute-done.47 = bf16[96,2048]{1,0:T(8,128)(2,1)S(1)} collective-permute-done((bf16[96,2048]{1,0:T(8,128)(2,1)S(1)}, bf16[96,2048]{1,0:T(8,128)(2,1)S(1)}, u32[]{:S(2)}, u32[]{:S(2)}) %collective-permute-start.47) | collective-permute-done | bytes 393248 | tf_op jit(solution)/shard_map/ppermute | solution.py:169
  (214 shorter events, 59.2 us)
Async XLA Ops:
  3.7 37.0 %all-to-all-start = ((bf16[8,96,768]{2,1,0:T(8,128)(2,1)}), bf16[8,96,768]{2,1,0:T(8,128)(2,1)S(1)}, u32[]{:S(2)}, u32[]{:S(2)}) async-start(bf16[8,96,768]{2,1,0:T(8,128)(2,1)} %pad_maximum_fusion), calls=%async_computation | async-start | bytes 2359296 | tf_op jit(solution)/shard_map/all_to_all | solution.py:148
  23.9 25.4 %collective-permute-start.16 = (f32[2,4,4,96]{3,2,1,0:T(4,128)S(1)}, f32[2,4,4,96]{3,2,1,0:T(4,128)S(1)}, u32[]{:S(2)}, u32[]{:S(2)}) collective-permute-start(f32[2,4,4,96]{3,2,1,0:T(4,128)S(1)} %pad_maximum_fusion.3), channel_id=1, source_target_pairs={{0,8},{4,12},{8,16},{12,20},{16,24},{20,28},{24,0},{28,4},{1,9},{5... | collective-permute-start | bytes 36872 | tf_op jit(solution)/shard_map/ppermute | solution.py:169
  27.5 21.9 %collective-permute-start.22 = (f32[2,4,4,96]{3,2,1,0:T(4,128)S(1)}, f32[2,4,4,96]{3,2,1,0:T(4,128)S(1)}, u32[]{:S(2)}, u32[]{:S(2)}) collective-permute-start(f32[2,4,4,96]{3,2,1,0:T(4,128)S(1)} %pad_maximum_fusion.3), channel_id=1, source_target_pairs={{0,16},{4,20},{8,24},{12,28},{16,0},{20,4},{24,8},{28,12},{1,17},{... | collective-permute-start | bytes 36872 | tf_op jit(solution)/shard_map/ppermute | solution.py:169
  29.5 34.8 %collective-permute-start.30 = (f32[2,4,4,96]{3,2,1,0:T(4,128)S(1)}, f32[2,4,4,96]{3,2,1,0:T(4,128)S(1)}, u32[]{:S(2)}, u32[]{:S(2)}) collective-permute-start(f32[2,4,4,96]{3,2,1,0:T(4,128)S(1)} %pad_maximum_fusion.3), channel_id=1, source_target_pairs={{0,24},{4,28},{8,0},{12,4},{16,8},{20,12},{24,16},{28,20},{1,25},{... | collective-permute-start | bytes 36872 | tf_op jit(solution)/shard_map/ppermute | solution.py:169
  45.6 15.1 %all-to-all-start.1 = ((bf16[8,96,256]{2,1,0:T(8,128)(2,1)}), bf16[8,96,256]{2,1,0:T(8,128)(2,1)S(1)}, u32[]{:S(2)}, u32[]{:S(2)}) async-start(bf16[8,96,256]{2,1,0:T(8,128)(2,1)} %bitcast.5), calls=%async_computation.1 | async-start | bytes 786432 | tf_op jit(solution)/shard_map/all_to_all | solution.py:150
  64.3 11.3 %collective-permute-start.2 = (bf16[96,2048]{1,0:T(8,128)(2,1)S(1)}, bf16[96,2048]{1,0:T(8,128)(2,1)S(1)}, u32[]{:S(2)}, u32[]{:S(2)}) collective-permute-start(bf16[96,2048]{1,0:T(8,128)(2,1)S(1)} %fusion.1), channel_id=1, source_target_pairs={{0,8},{4,12},{8,16},{12,20},{16,24},{20,28},{24,0},{28,4},{1,9},{5... | collective-permute-start | bytes 1179656 | tf_op jit(solution)/shard_map/ppermute | solution.py:169
  78.0 21.2 %collective-permute-start.6 = (bf16[96,2048]{1,0:T(8,128)(2,1)S(1)}, bf16[96,2048]{1,0:T(8,128)(2,1)S(1)}, u32[]{:S(2)}, u32[]{:S(2)}) collective-permute-start(bf16[96,2048]{1,0:T(8,128)(2,1)S(1)} %collective-permute-done.2), channel_id=1, source_target_pairs={{0,4},{4,0},{8,12},{12,8},{16,20},{20,16},{24,28},{28,24},{1,5},{5... | collective-permute-start | bytes 1179656 | tf_op jit(solution)/shard_map/ppermute | solution.py:165
  79.7 19.5 %collective-permute-start.7 = (bf16[96,2048]{1,0:T(8,128)(2,1)S(1)}, bf16[96,2048]{1,0:T(8,128)(2,1)S(1)}, u32[]{:S(2)}, u32[]{:S(2)}) collective-permute-start(bf16[96,2048]{1,0:T(8,128)(2,1)S(1)} %collective-permute-done.2), channel_id=1, source_target_pairs={{0,2},{1,3},{2,0},{3,1},{4,6},{5,7},{6,4},{7,5},{8,10},{9,11},{10,... | collective-permute-start | bytes 1179656 | tf_op jit(solution)/shard_map/ppermute | solution.py:161
  81.2 18.0 %collective-permute-start.10 = (bf16[96,2048]{1,0:T(8,128)(2,1)S(1)}, bf16[96,2048]{1,0:T(8,128)(2,1)S(1)}, u32[]{:S(2)}, u32[]{:S(2)}) collective-permute-start(bf16[96,2048]{1,0:T(8,128)(2,1)S(1)} %collective-permute-done.2), channel_id=1, source_target_pairs={{0,8},{4,12},{8,16},{12,20},{16,24},{20,28},{24,0},{28,4},{1,9},{5... | collective-permute-start | bytes 1179656 | tf_op jit(solution)/shard_map/ppermute | solution.py:169
  109.3 13.6 %collective-permute-start.14 = (bf16[384,2048]{1,0:T(8,128)(2,1)S(1)}, bf16[384,2048]{1,0:T(8,128)(2,1)S(1)}, u32[]{:S(2)}, u32[]{:S(2)}) collective-permute-start(bf16[384,2048]{1,0:T(8,128)(2,1)S(1)} %constant_dynamic-update-slice_fusion.5.rows_ref), channel_id=1, source_target_pairs={{0,1},{1,0},{2,3},{3,2},{4,5},{5,4},{6,7},{7,6},{8,9},{9,8},{10,11... | collective-permute-start | bytes 4718600 | tf_op jit(solution)/shard_map/ppermute | solution.py:157
  109.4 13.5 %collective-permute-start.17 = (bf16[96,2048]{1,0:T(8,128)(2,1)S(1)}, bf16[96,2048]{1,0:T(8,128)(2,1)S(1)}, u32[]{:S(2)}, u32[]{:S(2)}) collective-permute-start(bf16[96,2048]{1,0:T(8,128)(2,1)S(1)} %collective-permute-done.10), channel_id=1, source_target_pairs={{0,8},{4,12},{8,16},{12,20},{16,24},{20,28},{24,0},{28,4},{1,9},{5... | collective-permute-start | bytes 1179656 | tf_op jit(solution)/shard_map/ppermute | solution.py:169
  109.7 21.5 %collective-permute-start.18 = (bf16[192,2048]{1,0:T(8,128)(2,1)S(1)}, bf16[192,2048]{1,0:T(8,128)(2,1)S(1)}, u32[]{:S(2)}, u32[]{:S(2)}) collective-permute-start(bf16[192,2048]{1,0:T(8,128)(2,1)S(1)} %pad_maximum_fusion.1), channel_id=1, source_target_pairs={{0,2},{1,3},{2,0},{3,1},{4,6},{5,7},{6,4},{7,5},{8,10},{9,11},{10,... | collective-permute-start | bytes 2359304 | tf_op jit(solution)/shard_map/ppermute | solution.py:161
  133.6 11.2 %collective-permute-start.20 = (bf16[384,2048]{1,0:T(8,128)(2,1)S(1)}, bf16[384,2048]{1,0:T(8,128)(2,1)S(1)}, u32[]{:S(2)}, u32[]{:S(2)}) collective-permute-start(bf16[384,2048]{1,0:T(8,128)(2,1)S(1)} %gated_ffn.10), channel_id=1, source_target_pairs={{0,1},{1,0},{2,3},{3,2},{4,5},{5,4},{6,7},{7,6},{8,9},{9,8},{10,11... | collective-permute-start | bytes 4718600 | tf_op jit(solution)/shard_map/ppermute | solution.py:157
  133.8 11.1 %collective-permute-start.21 = (bf16[384,2048]{1,0:T(8,128)(2,1)S(1)}, bf16[384,2048]{1,0:T(8,128)(2,1)S(1)}, u32[]{:S(2)}, u32[]{:S(2)}) collective-permute-start(bf16[384,2048]{1,0:T(8,128)(2,1)S(1)} %constant_dynamic-update-slice_fusion.10.rows_ref), channel_id=1, source_target_pairs={{0,1},{1,0},{2,3},{3,2},{4,5},{5,4},{6,7},{7,6},{8,9},{9,8},{10,11... | collective-permute-start | bytes 4718600 | tf_op jit(solution)/shard_map/ppermute | solution.py:157
  135.3 20.6 %collective-permute-start.25 = (bf16[192,2048]{1,0:T(8,128)(2,1)}, bf16[192,2048]{1,0:T(8,128)(2,1)S(1)}, u32[]{:S(2)}, u32[]{:S(2)}) collective-permute-start(bf16[192,2048]{1,0:T(8,128)(2,1)} %pad_maximum_fusion.2), channel_id=1, source_target_pairs={{0,2},{1,3},{2,0},{3,1},{4,6},{5,7},{6,4},{7,5},{8,10},{9,11},{10,... | collective-permute-start | bytes 2359304 | tf_op jit(solution)/shard_map/ppermute | solution.py:161
  145.5 13.7 %collective-permute-start.23 = (bf16[48,2048]{1,0:T(8,128)(2,1)S(1)}, bf16[48,2048]{1,0:T(8,128)(2,1)S(1)}, u32[]{:S(2)}, u32[]{:S(2)}) collective-permute-start(bf16[48,2048]{1,0:T(8,128)(2,1)S(1)} %get-tuple-element.304), channel_id=1, source_target_pairs={{0,2},{1,3},{2,0},{3,1},{4,6},{5,7},{6,4},{7,5},{8,10},{9,11},{10,... | collective-permute-start | bytes 589832 | tf_op jit(solution)/shard_map/ppermute | solution.py:161
  146.1 13.1 %collective-permute-start.24 = (bf16[48,2048]{1,0:T(8,128)(2,1)S(1)}, bf16[48,2048]{1,0:T(8,128)(2,1)S(1)}, u32[]{:S(2)}, u32[]{:S(2)}) collective-permute-start(bf16[48,2048]{1,0:T(8,128)(2,1)S(1)} %get-tuple-element.303), channel_id=1, source_target_pairs={{0,4},{4,0},{8,12},{12,8},{16,20},{20,16},{24,28},{28,24},{1,5},{5... | collective-permute-start | bytes 589832 | tf_op jit(solution)/shard_map/ppermute | solution.py:165
  159.2 12.8 %collective-permute-start.26 = (bf16[384,2048]{1,0:T(8,128)(2,1)S(1)}, bf16[384,2048]{1,0:T(8,128)(2,1)S(1)}, u32[]{:S(2)}, u32[]{:S(2)}) collective-permute-start(bf16[384,2048]{1,0:T(8,128)(2,1)S(1)} %gated_ffn.12), channel_id=1, source_target_pairs={{0,1},{1,0},{2,3},{3,2},{4,5},{5,4},{6,7},{7,6},{8,9},{9,8},{10,11... | collective-permute-start | bytes 4718600 | tf_op jit(solution)/shard_map/ppermute | solution.py:157
  159.4 12.6 %collective-permute-start.29 = (bf16[384,2048]{1,0:T(8,128)(2,1)S(1)}, bf16[384,2048]{1,0:T(8,128)(2,1)S(1)}, u32[]{:S(2)}, u32[]{:S(2)}) collective-permute-start(bf16[384,2048]{1,0:T(8,128)(2,1)S(1)} %constant_dynamic-update-slice_fusion.13.rows_ref), channel_id=1, source_target_pairs={{0,1},{1,0},{2,3},{3,2},{4,5},{5,4},{6,7},{7,6},{8,9},{9,8},{10,11... | collective-permute-start | bytes 4718600 | tf_op jit(solution)/shard_map/ppermute | solution.py:157
  160.0 24.3 %collective-permute-start.5 = (bf16[384,2048]{1,0:T(8,128)(2,1)S(1)}, bf16[384,2048]{1,0:T(8,128)(2,1)S(1)}, u32[]{:S(2)}, u32[]{:S(2)}) collective-permute-start(bf16[384,2048]{1,0:T(8,128)(2,1)S(1)} %constant_dynamic-update-slice_fusion.rows_ref), channel_id=1, source_target_pairs={{0,1},{1,0},{2,3},{3,2},{4,5},{5,4},{6,7},{7,6},{8,9},{9,8},{10,11... | collective-permute-start | bytes 4718600 | tf_op jit(solution)/shard_map/ppermute | solution.py:157
  160.2 11.6 %collective-permute-start.27 = (bf16[96,2048]{1,0:T(8,128)(2,1)S(1)}, bf16[96,2048]{1,0:T(8,128)(2,1)S(1)}, u32[]{:S(2)}, u32[]{:S(2)}) collective-permute-start(bf16[96,2048]{1,0:T(8,128)(2,1)S(1)} %convert_element_type.181), channel_id=1, source_target_pairs={{0,4},{4,0},{8,12},{12,8},{16,20},{20,16},{24,28},{28,24},{1,5},{5... | collective-permute-start | bytes 1179656 | tf_op jit(solution)/shard_map/ppermute | solution.py:165
  160.7 11.3 %collective-permute-start.28 = (bf16[96,2048]{1,0:T(8,128)(2,1)S(1)}, bf16[96,2048]{1,0:T(8,128)(2,1)S(1)}, u32[]{:S(2)}, u32[]{:S(2)}) collective-permute-start(bf16[96,2048]{1,0:T(8,128)(2,1)S(1)} %convert_element_type.183), channel_id=1, source_target_pairs={{0,2},{1,3},{2,0},{3,1},{4,6},{5,7},{6,4},{7,5},{8,10},{9,11},{10,... | collective-permute-start | bytes 1179656 | tf_op jit(solution)/shard_map/ppermute | solution.py:161
  172.7 11.5 %collective-permute-start.31 = (bf16[48,2048]{1,0:T(8,128)(2,1)S(1)}, bf16[48,2048]{1,0:T(8,128)(2,1)S(1)}, u32[]{:S(2)}, u32[]{:S(2)}) collective-permute-start(bf16[48,2048]{1,0:T(8,128)(2,1)S(1)} %get-tuple-element.302), channel_id=1, source_target_pairs={{0,2},{1,3},{2,0},{3,1},{4,6},{5,7},{6,4},{7,5},{8,10},{9,11},{10,... | collective-permute-start | bytes 589832 | tf_op jit(solution)/shard_map/ppermute | solution.py:161
  184.3 12.2 %collective-permute-start.33 = (bf16[384,2048]{1,0:T(8,128)(2,1)S(1)}, bf16[384,2048]{1,0:T(8,128)(2,1)S(1)}, u32[]{:S(2)}, u32[]{:S(2)}) collective-permute-start(bf16[384,2048]{1,0:T(8,128)(2,1)S(1)} %gated_ffn.14), channel_id=1, source_target_pairs={{0,1},{1,0},{2,3},{3,2},{4,5},{5,4},{6,7},{7,6},{8,9},{9,8},{10,11... | collective-permute-start | bytes 4718600 | tf_op jit(solution)/shard_map/ppermute | solution.py:157
  184.5 11.6 %collective-permute-start.36 = (bf16[96,2048]{1,0:T(8,128)(2,1)S(1)}, bf16[96,2048]{1,0:T(8,128)(2,1)S(1)}, u32[]{:S(2)}, u32[]{:S(2)}) collective-permute-start(bf16[96,2048]{1,0:T(8,128)(2,1)S(1)} %add_convert_fusion.2), channel_id=1, source_target_pairs={{0,24},{4,28},{8,0},{12,4},{16,8},{20,12},{24,16},{28,20},{1,25},{... | collective-permute-start | bytes 1179656 | tf_op jit(solution)/shard_map/ppermute | solution.py:169
  184.7 11.6 %collective-permute-start.34 = (bf16[96,2048]{1,0:T(8,128)(2,1)S(1)}, bf16[96,2048]{1,0:T(8,128)(2,1)S(1)}, u32[]{:S(2)}, u32[]{:S(2)}) collective-permute-start(bf16[96,2048]{1,0:T(8,128)(2,1)S(1)} %convert_element_type.187), channel_id=1, source_target_pairs={{0,4},{4,0},{8,12},{12,8},{16,20},{20,16},{24,28},{28,24},{1,5},{5... | collective-permute-start | bytes 1179656 | tf_op jit(solution)/shard_map/ppermute | solution.py:165
  185.2 11.3 %collective-permute-start.35 = (bf16[96,2048]{1,0:T(8,128)(2,1)S(1)}, bf16[96,2048]{1,0:T(8,128)(2,1)S(1)}, u32[]{:S(2)}, u32[]{:S(2)}) collective-permute-start(bf16[96,2048]{1,0:T(8,128)(2,1)S(1)} %convert_element_type.189), channel_id=1, source_target_pairs={{0,2},{1,3},{2,0},{3,1},{4,6},{5,7},{6,4},{7,5},{8,10},{9,11},{10,... | collective-permute-start | bytes 1179656 | tf_op jit(solution)/shard_map/ppermute | solution.py:161
  200.1 25.4 %collective-permute-start.46 = (bf16[96,2048]{1,0:T(8,128)(2,1)S(1)}, bf16[96,2048]{1,0:T(8,128)(2,1)S(1)}, u32[]{:S(2)}, u32[]{:S(2)}) collective-permute-start(bf16[96,2048]{1,0:T(8,128)(2,1)S(1)} %add_convert_fusion.1), channel_id=1, source_target_pairs={{0,16},{4,20},{8,24},{12,28},{16,0},{20,4},{24,8},{28,12},{1,17},{... | collective-permute-start | bytes 1179656 | tf_op jit(solution)/shard_map/ppermute | solution.py:169
  205.3 16.3 %collective-permute-start.40 = (bf16[96,2048]{1,0:T(8,128)(2,1)S(1)}, bf16[96,2048]{1,0:T(8,128)(2,1)S(1)}, u32[]{:S(2)}, u32[]{:S(2)}) collective-permute-start(bf16[96,2048]{1,0:T(8,128)(2,1)S(1)} %convert_element_type.196), channel_id=1, source_target_pairs={{0,4},{4,0},{8,12},{12,8},{16,20},{20,16},{24,28},{28,24},{1,5},{5... | collective-permute-start | bytes 1179656 | tf_op jit(solution)/shard_map/ppermute | solution.py:165
  207.2 14.4 %collective-permute-start.41 = (bf16[96,2048]{1,0:T(8,128)(2,1)S(1)}, bf16[96,2048]{1,0:T(8,128)(2,1)S(1)}, u32[]{:S(2)}, u32[]{:S(2)}) collective-permute-start(bf16[96,2048]{1,0:T(8,128)(2,1)S(1)} %convert_element_type.198), channel_id=1, source_target_pairs={{0,2},{1,3},{2,0},{3,1},{4,6},{5,7},{6,4},{7,5},{8,10},{9,11},{10,... | collective-permute-start | bytes 1179656 | tf_op jit(solution)/shard_map/ppermute | solution.py:161
  209.2 12.4 %collective-permute-start.42 = (bf16[48,2048]{1,0:T(8,128)(2,1)S(1)}, bf16[48,2048]{1,0:T(8,128)(2,1)S(1)}, u32[]{:S(2)}, u32[]{:S(2)}) collective-permute-start(bf16[48,2048]{1,0:T(8,128)(2,1)S(1)} %get-tuple-element.298), channel_id=1, source_target_pairs={{0,2},{1,3},{2,0},{3,1},{4,6},{5,7},{6,4},{7,5},{8,10},{9,11},{10,... | collective-permute-start | bytes 589832 | tf_op jit(solution)/shard_map/ppermute | solution.py:161
  210.0 11.6 %collective-permute-start.43 = (bf16[48,2048]{1,0:T(8,128)(2,1)S(1)}, bf16[48,2048]{1,0:T(8,128)(2,1)S(1)}, u32[]{:S(2)}, u32[]{:S(2)}) collective-permute-start(bf16[48,2048]{1,0:T(8,128)(2,1)S(1)} %get-tuple-element.297), channel_id=1, source_target_pairs={{0,4},{4,0},{8,12},{12,8},{16,20},{20,16},{24,28},{28,24},{1,5},{5... | collective-permute-start | bytes 589832 | tf_op jit(solution)/shard_map/ppermute | solution.py:165
  (26 other events, 203.3 us)
